TPU v7x, 256 devices: a whole 4x4x8 slice. The times are simulated.
256 devices in a mesh: row: 8 (over z_hi, core), col: 32 (over z_lo, y, x).
Axes of the slice: x: 4, y: 4, z: 8 (z_hi: 4, z_lo: 2; z = z_hi * 2 + z_lo), core: 2. Of those that a mesh axis runs over, the one named last changes fastest.
Arguments:
- object_in: float32 [2, 2, 2048, 8192], P(None, None, 'row', 'col'), may hold values from -4 to 4
- probe_in: float32 [2, 256, 256], replicated, may hold values from -5 to 5
- positions: int32 [8, 32, 2, 2], P('row', 'col'), may hold values from -32 to 32
- intensity: float32 [8, 32, 2, 256, 256], P('row', 'col'), may hold values from 0.1 to 8.2
Outputs:
- object_out: float32 [2, 2, 2048, 8192], P(None, None, 'row', 'col')
- probe_out: float32 [2, 256, 256], replicated
Inputs may be any that keep to these rules, and one draw needn't show every extreme that they name: positions[r, c, p] = (dy, dx) places the probe of position p on object rows r * 256 + dy to r * 256 + dy + 255 and columns c * 256 + dx to c * 256 + dx + 255.
All inputs are finite; a program needn't handle non-finite values.
Results may differ from a plain program's by a relative error of at most 0.0003.
Values sent between devices are 32-bit elements; how exact they have to be, the bound alone decides.
A program may use at most 64 MiB of HBM per device.

v0:
```python
import math
import jax
import jax.numpy as jnp
from jax import lax
from jax.sharding import Mesh
from jax.sharding import PartitionSpec as P

RIM = 32
COL = ("col_0", "col_1", "col_2")
ROW = ("row_0", "row_1")
ROW_COL = ("row_0", "row_1", "col_0", "col_1", "col_2")


def passed_along(value, axis, steps):
    count = lax.axis_size(axis)
    initial, last = (max(0, -steps), min(count, count - steps))
    return lax.ppermute(value, axis, [(source, source + steps) for source in range(initial, last)])


def extended(cells, sides, width):
    for axis, dim in sides:
        count = lax.axis_size(axis)
        ends = count - 1
        head = lax.slice_in_dim(cells, 0, width, axis=dim)
        tail = lax.slice_in_dim(cells, cells.shape[dim] - width, cells.shape[dim], axis=dim)
        cells = jnp.concatenate(
            [
                lax.ppermute(tail, axis, [(i, (i + 1) % count) for i in range(ends)]),
                cells,
                lax.ppermute(head, axis, [((i + 1) % count, i) for i in range(ends)]),
            ],
            axis=dim,
        )
    return cells


def by_axis(array, axes):
    for axis in axes:
        array = lax.psum(array, axis)
    return array


def one_axis_at_a_time(array, axes):
    for axis in axes:
        array = lax.pmax(array, axis)
    return array


def tables(extent):
    line_idx = jnp.arange(extent, dtype=jnp.int32)
    turn_count = line_idx[:, None] * line_idx[None, :] % extent
    angles = turn_count.astype(jnp.float32) * (2.0 * math.pi / extent)
    factor = 1.0 / math.sqrt(extent)
    cosine = jnp.cos(angles) * factor
    sine_tab = jnp.sin(angles) * factor
    frequency = ((line_idx + extent // 2) % extent - extent // 2).astype(jnp.float32)
    phases = (
        -math.pi * 8.0 / (extent * extent) * (frequency[:, None] ** 2 + frequency[None, :] ** 2)
    )
    return (cosine, sine_tab, jnp.cos(phases), jnp.sin(phases))


def matrices(cosine, sine_tab, orient):
    return (cosine, sine_tab, float(orient))


def transform(real_part, imag_part, tables_pair):
    cosine, sine_tab, orient = tables_pair
    high = lax.Precision.HIGHEST
    rc = jnp.einsum("byx,xk->byk", real_part, cosine, precision=high)
    rs = jnp.einsum("byx,xk->byk", real_part, sine_tab, precision=high)
    ic = jnp.einsum("byx,xk->byk", imag_part, cosine, precision=high)
    isn = jnp.einsum("byx,xk->byk", imag_part, sine_tab, precision=high)
    mid_re = rc + orient * isn
    mid_im = ic - orient * rs
    out_re = jnp.einsum("ky,byx->bkx", cosine, mid_re, precision=high) + orient * jnp.einsum(
        "ky,byx->bkx", sine_tab, mid_im, precision=high
    )
    out_im = jnp.einsum("ky,byx->bkx", cosine, mid_im, precision=high) - orient * jnp.einsum(
        "ky,byx->bkx", sine_tab, mid_re, precision=high
    )
    return (out_re, out_im)


def times_plain(first_re, first_im, second_re, second_im):
    return (
        first_re * second_re - first_im * second_im,
        first_re * second_im + first_im * second_re,
    )


def times_conj(first_re, first_im, second_re, second_im):
    return (
        first_re * second_re + first_im * second_im,
        first_re * second_im - first_im * second_re,
    )


def tile_gradient(window, probe, offsets, measured, constants):
    cosine, sine_tab, kern_re, kern_im = constants
    forward = matrices(cosine, sine_tab, 1)
    backward = matrices(cosine, sine_tab, -1)
    extent = probe.shape[-1]
    zero_idx = jnp.zeros((), jnp.int32)

    def cut_patch(offset):
        return lax.dynamic_slice(
            window, (zero_idx, zero_idx, offset[0] + RIM, offset[1] + RIM), (2, 2, extent, extent)
        )

    patches = jax.vmap(cut_patch)(offsets)
    first_re, first_im = (patches[:, 0, 0], patches[:, 0, 1])
    second_re, second_im = (patches[:, 1, 0], patches[:, 1, 1])
    probe_re, probe_im = (probe[0], probe[1])
    wave_re, wave_im = times_plain(probe_re, probe_im, first_re, first_im)
    spec_re, spec_im = transform(wave_re, wave_im, forward)
    spec_re, spec_im = times_plain(kern_re, kern_im, spec_re, spec_im)
    prop_re, prop_im = transform(spec_re, spec_im, backward)
    exit_re, exit_im = times_plain(prop_re, prop_im, second_re, second_im)
    far_re, far_im = transform(exit_re, exit_im, forward)
    excess = 2.0 * (far_re * far_re + far_im * far_im - measured)
    back_re, back_im = transform(excess * far_re, excess * far_im, backward)
    grad2_re, grad2_im = times_conj(prop_re, prop_im, back_re, back_im)
    lift_re, lift_im = times_conj(second_re, second_im, back_re, back_im)
    lift_re, lift_im = transform(lift_re, lift_im, forward)
    lift_re, lift_im = times_conj(kern_re, kern_im, lift_re, lift_im)
    enter_re, enter_im = transform(lift_re, lift_im, backward)
    grad1_re, grad1_im = times_conj(probe_re, probe_im, enter_re, enter_im)
    probe_re_g, probe_im_g = times_conj(first_re, first_im, enter_re, enter_im)
    probe_grad = jnp.stack([jnp.sum(probe_re_g, 0), jnp.sum(probe_im_g, 0)], 0)
    pieces = jnp.stack([jnp.stack([grad1_re, grad1_im], 1), jnp.stack([grad2_re, grad2_im], 1)], 1)
    gradient = jnp.zeros(window.shape, jnp.float32)
    for position in range(offsets.shape[0]):
        start_at = (zero_idx, zero_idx, offsets[position, 0] + RIM, offsets[position, 1] + RIM)
        current = lax.dynamic_slice(gradient, start_at, pieces.shape[1:])
        gradient = lax.dynamic_update_slice(gradient, current + pieces[position], start_at)
    return (gradient, probe_grad)


def turned(block):
    return jnp.swapaxes(block, 2, 3)


def cols_then_rows(gradient):
    inner_px = gradient.shape[-1] - 2 * RIM
    upper_end = RIM + inner_px
    from_right = turned(passed_along(turned(gradient[..., :RIM]), COL, -1))
    from_left = turned(passed_along(turned(gradient[..., upper_end:]), COL, 1))
    middle = gradient[..., RIM:upper_end]
    middle = middle.at[..., inner_px - RIM :].add(from_right)
    middle = middle.at[..., :RIM].add(from_left)
    from_below = passed_along(middle[:, :, :RIM, :], ROW, -1)
    from_above = passed_along(middle[:, :, upper_end:, :], ROW, 1)
    interior = middle[:, :, RIM:upper_end, :]
    interior = interior.at[:, :, inner_px - RIM :, :].add(from_below)
    interior = interior.at[:, :, :RIM, :].add(from_above)
    return interior


def local(object_in, probe_in, positions, intensity):
    extent = probe_in.shape[-1]
    constants = tables(extent)
    offsets = positions.reshape(-1, 2)
    measured = intensity.reshape(-1, extent, extent)
    tile_total = lax.axis_size(ROW) * lax.axis_size(COL)
    probe_rate = 2.0 / tile_total
    current = object_in
    window = extended(current, ((ROW, 2), (COL, 3)), RIM)
    gradient, probe_grad = tile_gradient(window, probe_in, offsets, measured, constants)
    probe_total = by_axis(probe_grad, ROW_COL)
    probe_next = probe_in - probe_rate * probe_total
    descent = cols_then_rows(gradient)
    local_peak = jnp.max(descent[:, 0] ** 2 + descent[:, 1] ** 2)
    largest = one_axis_at_a_time(local_peak, ROW_COL)
    current = current - 0.3 * descent / (jnp.sqrt(largest) + 1e-06)
    return (current, probe_next)


def solution(mesh):
    torus = Mesh(mesh.devices.reshape(4, 2, 2, 4, 4), ("row_0", "row_1", "col_0", "col_1", "col_2"))
    placed = (P(None, None, ROW, COL), P(), P(ROW, COL, None, None), P(ROW, COL, None, None, None))
    return jax.shard_map(
        local,
        mesh=torus,
        in_specs=placed,
        out_specs=(P(None, None, ROW, COL), P()),
        check_vma=False,
    )
```

profile of v0, /device:TPU:8, one launch (start us, length us, event | category | flops | bytes accessed | tf_op | source)
XLA Modules:
  0.0 397.1 jit_solution(860421095637435779)
XLA Ops:
  16.1 2.1 copy.98
  19.2 3.4 collective-permute-start.2
  22.7 4.6 %collective-permute-start.3 = (f32[2,2,320,32]{2,3,1,0:T(8,128)S(1)}, f32[2,2,320,32]{2,3,1,0:T(8,128)S(1)}, u32[]{:S(2)}, u32[]{:S(2)}) collective-permute-start(f32[2,2,320,32]{2,3,1,0:T(8,128)S(1)} %get-tuple-element.85), channel_id=1, source_target_pairs={{1,0},{2,1},{3,2},{4,3},{5,4},{6,5},{7,6},{8,7},{9,8},{10,9},{11,1... | collective-permute-start | bytes 491528 | tf_op jit(solution)/shard_map/ppermute | solution.py:30
  32.2 11.2 %while.5 = (s32[]{:T(128)}, f32[2,2,320,320]{2,3,1,0:T(8,128)S(1)}, s32[2,4]{1,0:T(2,128)S(1)}, f32[2,2,2,256,256]{3,4,0,2,1:T(8,128)}, s32[]{:T(128)}) while((s32[]{:T(128)}, f32[2,2,320,320]{2,3,1,0:T(8,128)S(1)}, s32[2,4]{1,0:T(2,128)S(1)}, f32[2,2,2,256,256]{3,4,0,2,1:T(8,128)}, s32[]{:T(128)}) %tuple.62), condition=%wide.while_cond.4, body=%wide.while_body.4.sunk | while | flops 2 | bytes 21496496 | solution.py:107
  43.4 3.4 fusion.112
  46.8 3.2 fusion.116
  57.5 2.3 fusion.22
  69.1 2.1 fusion.20
  80.4 2.1 convolution_add_fusion.3
  93.5 2.3 fusion.88
  97.8 1.9 fusion.12
  105.3 2.1 add_bitcast_fusion
  116.7 2.1 fusion.82
  128.1 2.3 fusion.4
  135.9 2.0 fusion.38
  145.6 65.6 %all-reduce.6.cloned.1.call-done = f32[2,256,256]{1,2,0:T(8,128)} async-done(((f32[2,256,256]{1,2,0:T(8,128)}), f32[2,256,256]{1,2,0:T(8,128)}) %all-reduce.6.cloned.1.call-update) | async-done | bytes 524304 | tf_op jit(solution)/shard_map/psum | solution.py:39
  211.3 2.1 fusion.25
  213.6 14.1 %dynamic_update_slice.6 = f32[2,2,320,320]{2,3,1,0:T(8,128)S(1)} dynamic-update-slice(f32[2,2,320,320]{2,3,1,0:T(8,128)S(1)} %broadcast_in_dim.2, f32[2,2,256,256]{2,3,1,0:T(8,128)} %fusion.25, s32[]{:T(128)} %constant.162.clone.1, s32[]{:T(128)} %constant.162.clone.1, s32[]{:T(128)S(6)} %select_n.155, s32[]{:T(128)S(6)} %select_n.156) | dynamic-update-slice | bytes 2097156 | tf_op jit(solution)/shard_map/dynamic_update_slice | solution.py:136
  227.7 2.4 fusion.27
  230.1 13.8 %dynamic_update_slice.7 = f32[2,2,320,320]{2,3,1,0:T(8,128)S(1)} dynamic-update-slice(f32[2,2,320,320]{2,3,1,0:T(8,128)S(1)} %dynamic_update_slice.6, f32[2,2,256,256]{2,3,1,0:T(8,128)} %fusion.27, s32[]{:T(128)} %constant.162.clone.1, s32[]{:T(128)} %constant.162.clone.1, s32[]{:T(128)S(6)} %select_n.157, s32[]{:T(128)S(6)} %select_n.158) | dynamic-update-slice | bytes 2097156 | tf_op jit(solution)/shard_map/dynamic_update_slice | solution.py:136
  244.7 4.0 %collective-permute-start.4 = (f32[2,2,32,320]{3,2,1,0:T(8,128)}, f32[2,2,32,320]{3,2,1,0:T(8,128)}, u32[]{:S(2)}, u32[]{:S(2)}) collective-permute-start(f32[2,2,32,320]{3,2,1,0:T(8,128)} %get-tuple-element.87), channel_id=1, source_target_pairs={{1,0},{2,1},{3,2},{4,3},{5,4},{6,5},{7,6},{8,7},{9,8},{10,9},{11,1... | collective-permute-start | bytes 491528 | tf_op jit(solution)/shard_map/ppermute | solution.py:17
  253.5 5.9 %collective-permute-done.5 = f32[2,2,32,320]{3,2,1,0:T(8,128)S(1)} collective-permute-done((f32[2,2,32,320]{3,2,1,0:T(8,128)S(1)}, f32[2,2,32,320]{3,2,1,0:T(8,128)S(1)}, u32[]{:S(2)}, u32[]{:S(2)}) %collective-permute-start.5) | collective-permute-done | bytes 163872 | tf_op jit(solution)/shard_map/ppermute | solution.py:17
  259.5 27.1 %all-reduce.10.cloned.1.call-done = f32[2,256,256]{1,2,0:T(8,128)} async-done(((f32[2,256,256]{1,2,0:T(8,128)}), f32[2,256,256]{1,2,0:T(8,128)}) %all-reduce.10.cloned.1.call-update) | async-done | bytes 524304 | tf_op jit(solution)/shard_map/psum | solution.py:39
  289.2 3.9 collective-permute-start.7
  293.1 2.6 scatter-add.16
  295.7 40.5 %all-reduce.12.cloned.1.call-done = f32[2,256,256]{1,2,0:T(8,128)} async-done(((f32[2,256,256]{1,2,0:T(8,128)}), f32[2,256,256]{1,2,0:T(8,128)}) %all-reduce.12.cloned.1.call-update) | async-done | bytes 524304 | tf_op jit(solution)/shard_map/psum | solution.py:39
  337.4 2.3 scatter-add.19
  340.5 13.4 %pmax.35 = f32[]{:T(128)} all-reduce(f32[]{:T(128)} %fusion.29), channel_id=1, replica_groups=mesh['row_0'=4,'row_1'=2,'col_0'=2,'col_1'=4,'col_2'=4] {'row_0'}, use_global_device_ids=true, to_apply=%region_1.2 | all-reduce | flops 1 | bytes 8 | tf_op jit(solution)/shard_map/pmax | solution.py:45
  353.8 3.1 pmax.36
  356.9 5.5 %pmax.37 = f32[]{:T(128)} all-reduce(f32[]{:T(128)} %pmax.36), channel_id=1, replica_groups=mesh['row_0'=4,'row_1'=2,'col_0'=2,'col_1'=4,'col_2'=4] {'col_0'}, use_global_device_ids=true, to_apply=%region_3.4 | all-reduce | flops 1 | bytes 8 | tf_op jit(solution)/shard_map/pmax | solution.py:45
  362.4 10.0 %pmax.38 = f32[]{:T(128)} all-reduce(f32[]{:T(128)} %pmax.37), channel_id=1, replica_groups=mesh['row_0'=4,'row_1'=2,'col_0'=2,'col_1'=4,'col_2'=4] {'col_1'}, use_global_device_ids=true, to_apply=%region_4.5 | all-reduce | flops 1 | bytes 8 | tf_op jit(solution)/shard_map/pmax | solution.py:45
  373.4 11.1 %pmax.39 = f32[]{:T(128)} all-reduce(f32[]{:T(128)} %pmax.38), channel_id=1, replica_groups=mesh['row_0'=4,'row_1'=2,'col_0'=2,'col_1'=4,'col_2'=4] {'col_2'}, use_global_device_ids=true, to_apply=%region_5.6 | all-reduce | flops 1 | bytes 8 | tf_op jit(solution)/shard_map/pmax | solution.py:45
  (139 shorter events, 113.2 us)
Async XLA Ops:
  7.2 6.2 %copy-start.11 = (f32[2,256,256]{2,1,0:T(8,128)S(1)}, f32[2,256,256]{2,1,0:T(8,128)}, u32[]{:S(2)}) copy-start(f32[2,256,256]{2,1,0:T(8,128)} %param.13) | copy-start | bytes 1572868
  7.2 204.0 %all-reduce.6.cloned.1.call-start = ((), (), s32[]{:S(2)}) async-start(), calls=%async_computation | async-start | bytes 1048576 | tf_op jit(solution)/shard_map/psum | solution.py:39
  8.8 21.6 %copy-start.2 = (f32[2,2,256,256]{2,3,1,0:T(8,128)}, f32[2,2,256,256]{2,3,1,0:T(8,128)S(1)}, u32[]{:S(2)}) copy-start(f32[2,2,256,256]{2,3,1,0:T(8,128)S(1)} %copy.124) | copy-start | bytes 3145732
  10.1 8.1 %copy-start.14 = (s32[1,1,2,2]{3,2,1,0:T(2,128)S(1)}, s32[1,1,2,2]{3,2,1,0:T(2,128)}, u32[]{:S(2)}) copy-start(s32[1,1,2,2]{3,2,1,0:T(2,128)} %param.14) | copy-start | bytes 52
  10.1 8.2 %collective-permute-start = (f32[2,2,32,256]{2,3,1,0:T(8,128)}, f32[2,2,32,256]{2,3,1,0:T(8,128)S(1)}, u32[]{:S(2)}, u32[]{:S(2)}) collective-permute-start(f32[2,2,32,256]{2,3,1,0:T(8,128)} %get-tuple-element.96), channel_id=1, source_target_pairs={{0,32},{32,64},{64,96},{96,128},{128,160},{160,192},{192,224},{1,3... | collective-permute-start | bytes 393224 | tf_op jit(solution)/shard_map/ppermute | solution.py:28
  12.0 7.0 %collective-permute-start.1 = (f32[2,2,32,256]{2,3,1,0:T(8,128)}, f32[2,2,32,256]{2,3,1,0:T(8,128)S(1)}, u32[]{:S(2)}, u32[]{:S(2)}) collective-permute-start(f32[2,2,32,256]{2,3,1,0:T(8,128)} %get-tuple-element.97), channel_id=1, source_target_pairs={{32,0},{64,32},{96,64},{128,96},{160,128},{192,160},{224,192},{33,... | collective-permute-start | bytes 393224 | tf_op jit(solution)/shard_map/ppermute | solution.py:30
  18.3 10.7 %copy-start.8 = (f32[2,2,32,256]{2,3,1,0:T(8,128)}, f32[2,2,32,256]{2,3,1,0:T(8,128)S(1)}, u32[]{:S(2)}) copy-start(f32[2,2,32,256]{2,3,1,0:T(8,128)S(1)} %collective-permute-done) | copy-start | bytes 393220
  19.0 9.9 %copy-start.9 = (f32[2,2,32,256]{2,3,1,0:T(8,128)}, f32[2,2,32,256]{2,3,1,0:T(8,128)S(1)}, u32[]{:S(2)}) copy-start(f32[2,2,32,256]{2,3,1,0:T(8,128)S(1)} %collective-permute-done.1) | copy-start | bytes 393220
  19.2 9.7 %collective-permute-start.2 = (f32[2,2,320,32]{2,3,1,0:T(8,128)S(1)}, f32[2,2,320,32]{2,3,1,0:T(8,128)S(1)}, u32[]{:S(2)}, u32[]{:S(2)}) collective-permute-start(f32[2,2,320,32]{2,3,1,0:T(8,128)S(1)} %get-tuple-element.84), channel_id=1, source_target_pairs={{0,1},{1,2},{2,3},{3,4},{4,5},{5,6},{6,7},{7,8},{8,9},{9,10},{10,1... | collective-permute-start | bytes 491528 | tf_op jit(solution)/shard_map/ppermute | solution.py:28
  22.7 7.7 %collective-permute-start.3 = (f32[2,2,320,32]{2,3,1,0:T(8,128)S(1)}, f32[2,2,320,32]{2,3,1,0:T(8,128)S(1)}, u32[]{:S(2)}, u32[]{:S(2)}) collective-permute-start(f32[2,2,320,32]{2,3,1,0:T(8,128)S(1)} %get-tuple-element.85), channel_id=1, source_target_pairs={{1,0},{2,1},{3,2},{4,3},{5,4},{6,5},{7,6},{8,7},{9,8},{10,9},{11,1... | collective-permute-start | bytes 491528 | tf_op jit(solution)/shard_map/ppermute | solution.py:30
  32.2 1.3 copy-start
  35.7 1.9 copy-start.1
  37.7 1.3 copy-start
  41.2 1.9 copy-start.1
  43.4 6.6 %copy-start.5 = (f32[256,256]{0,1:T(8,128)S(1)}, f32[256,256]{0,1:T(8,128)}, u32[]{:S(2)}) copy-start(f32[256,256]{0,1:T(8,128)} %copy.64) | copy-start | bytes 786436
  43.4 6.6 %copy-start.6 = (f32[256,256]{0,1:T(8,128)S(1)}, f32[256,256]{0,1:T(8,128)}, u32[]{:S(2)}) copy-start(f32[256,256]{0,1:T(8,128)} %copy.71) | copy-start | bytes 786436
  43.4 6.6 %copy-start.7 = (f32[2,2,2,256,256]{3,4,0,2,1:T(8,128)S(1)}, f32[2,2,2,256,256]{3,4,0,2,1:T(8,128)}, u32[]{:S(2)}) copy-start(f32[2,2,2,256,256]{3,4,0,2,1:T(8,128)} %get-tuple-element.57) | copy-start | bytes 6291460
  86.1 5.5 %copy-start.4 = (f32[1,1,2,256,256]{3,4,2,1,0:T(8,128)S(1)}, f32[1,1,2,256,256]{3,4,2,1,0:T(8,128)}, u32[]{:S(2)}) copy-start(f32[1,1,2,256,256]{3,4,2,1,0:T(8,128)} %copy.98) | copy-start | bytes 1572868
  138.8 110.0 %all-reduce.8.cloned.1.call-start = ((), (), s32[]{:S(2)}) async-start(), calls=%async_computation.1 | async-start | bytes 1048576 | tf_op jit(solution)/shard_map/psum | solution.py:39
  211.2 75.3 %all-reduce.10.cloned.1.call-start = ((), (), s32[]{:S(2)}) async-start(), calls=%async_computation.2 | async-start | bytes 1048576 | tf_op jit(solution)/shard_map/psum | solution.py:39
  244.7 7.9 %collective-permute-start.4 = (f32[2,2,32,320]{3,2,1,0:T(8,128)}, f32[2,2,32,320]{3,2,1,0:T(8,128)}, u32[]{:S(2)}, u32[]{:S(2)}) collective-permute-start(f32[2,2,32,320]{3,2,1,0:T(8,128)} %get-tuple-element.87), channel_id=1, source_target_pairs={{1,0},{2,1},{3,2},{4,3},{5,4},{6,5},{7,6},{8,7},{9,8},{10,9},{11,1... | collective-permute-start | bytes 491528 | tf_op jit(solution)/shard_map/ppermute | solution.py:17
  248.8 87.5 %all-reduce.12.cloned.1.call-start = ((), (), s32[]{:S(2)}) async-start(), calls=%async_computation.3 | async-start | bytes 1048576 | tf_op jit(solution)/shard_map/psum | solution.py:39
  248.8 0.9 copy-start.13
  249.7 9.7 %collective-permute-start.5 = (f32[2,2,32,320]{3,2,1,0:T(8,128)S(1)}, f32[2,2,32,320]{3,2,1,0:T(8,128)S(1)}, u32[]{:S(2)}, u32[]{:S(2)}) collective-permute-start(f32[2,2,32,320]{3,2,1,0:T(8,128)S(1)} %copy-done.13), channel_id=1, source_target_pairs={{0,1},{1,2},{2,3},{3,4},{4,5},{5,6},{6,7},{7,8},{8,9},{9,10},{10,1... | collective-permute-start | bytes 491528 | tf_op jit(solution)/shard_map/ppermute | solution.py:17
  286.6 101.7 %all-reduce.14.cloned.1.call-start = ((), (), s32[]{:S(2)}) async-start(), calls=%async_computation.4 | async-start | bytes 1048576 | tf_op jit(solution)/shard_map/psum | solution.py:39
  287.6 5.5 %collective-permute-start.6 = (f32[2,2,32,256]{2,3,1,0:T(8,128)S(1)}, f32[2,2,32,256]{2,3,1,0:T(8,128)S(1)}, u32[]{:S(2)}, u32[]{:S(2)}) collective-permute-start(f32[2,2,32,256]{2,3,1,0:T(8,128)S(1)} %get-tuple-element.89), channel_id=1, source_target_pairs={{32,0},{64,32},{96,64},{128,96},{160,128},{192,160},{224,192},{33,... | collective-permute-start | bytes 393224 | tf_op jit(solution)/shard_map/ppermute | solution.py:17
  289.2 47.0 %collective-permute-start.7 = (f32[2,2,32,256]{2,3,1,0:T(8,128)}, f32[2,2,32,256]{2,3,1,0:T(8,128)}, u32[]{:S(2)}, u32[]{:S(2)}) collective-permute-start(f32[2,2,32,256]{2,3,1,0:T(8,128)} %get-tuple-element.88), channel_id=1, source_target_pairs={{0,32},{32,64},{64,96},{96,128},{128,160},{160,192},{192,224},{1,3... | collective-permute-start | bytes 393224 | tf_op jit(solution)/shard_map/ppermute | solution.py:17
  336.3 36.1 %copy-start.12 = (f32[2,256,256]{2,1,0:T(8,128)S(1)}, f32[2,256,256]{2,1,0:T(8,128)}, u32[]{:S(2)}) copy-start(f32[2,256,256]{2,1,0:T(8,128)} %param.13) | copy-start | bytes 1572868
  337.4 47.8 %copy-start.3 = (f32[2,2,256,256]{2,3,1,0:T(8,128)S(1)}, f32[2,2,256,256]{2,3,1,0:T(8,128)}, u32[]{:S(2)}) copy-start(f32[2,2,256,256]{2,3,1,0:T(8,128)} %copy-done.2) | copy-start | bytes 3145732
  385.4 2.9 copy-start.10
Sparse Core Ops, SparseCore 0:
  138.9 72.2 all-reduce.5
  213.8 28.7 all-reduce.7
  248.9 37.5 all-reduce.9
  288.7 47.4 all-reduce.11
  338.4 49.8 all-reduce.13
where the time goes:
time: 402 us; the launch traced here: 397 us
  waiting for transfers between devices  146 us (36%)
  matrix products  94.1 us (23%)
  local copies, waits for them, and re-layouts  57.4 us (14%)
  blocking collectives  43 us (11%)
  starting transfers between devices  22.4 us (6%)
  between operations  20.4 us (5%)
  other arithmetic  13.9 us (3%)
    psum x5, waiting for transfers between devices, by_axis(): array = lax.psum(array, axis)  135 us
    pmax x5, blocking collectives, one_axis_at_a_time(): array = lax.pmax(array, axis)  43 us
    dynamic_update_slice x2, local copies, waits for them, and re-layouts, tile_gradient(): lax.dynamic_update_slice(gradient, current + pieces[position], start_at)  27.9 us
    dot_general x6, matrix products, transform(): ic = jnp.einsum('byx,xk->byk', imag_part, cosine, precision=high)  13.1 us
    dot_general x6, matrix products, transform(): rc = jnp.einsum('byx,xk->byk', real_part, cosine, precision=high)  12.6 us
    dot_general x6, matrix products, transform(): rs = jnp.einsum('byx,xk->byk', real_part, sine_tab, precision=high)  11.8 us
    dot_general x6, matrix products, transform(): jnp.einsum('ky,byx->bkx', sine_tab, mid_im, precision=high)  11.5 us
    dot_general x6, matrix products, transform(): isn = jnp.einsum('byx,xk->byk', imag_part, sine_tab, precision=high)  11.5 us
  transfers between devices with their start and end apart: 13, of which 9 were waited for; matrix products, arithmetic and copies ran while one was open for 13% of the time, Pallas kernels for 0%

commit v1 on v0

--- a/solution.py
+++ b/solution.py
@@ -36,7 +36,7 @@
 
 def by_axis(array, axes):
     for axis in axes:
-        array = lax.psum(array, axis)
+        array = jnp.sum(lax.all_gather(array, axis), axis=0)
     return array
 
 

time: 402 us -> 428 us (1.065)
  waiting for transfers between devices: 146 us -> 156 us
  blocking collectives: 43 us -> 51.8 us
  other arithmetic: 13.9 us -> 20.1 us
    all_gather x0 -> x5, waiting for transfers between devices: none -> 143 us  [by_axis(): array = jnp.sum(lax.all_gather(array, axis), axis=0)]
    psum x5 -> x0, waiting for transfers between devices: 135 us -> none  [by_axis(): array = lax.psum(array, axis)]
    reduce_sum x0 -> x5, other arithmetic: none -> 11.3 us  [by_axis(): array = jnp.sum(lax.all_gather(array, axis), axis=0)]
    pmax x5, blocking collectives: 43 us -> 51.8 us  [one_axis_at_a_time(): array = lax.pmax(array, axis)]
  transfers between devices with their start and end apart: 13 -> 13, of which waited for: 9 -> 9; matrix products, arithmetic and copies ran while one was open for 13% -> 11% of each run, Pallas kernels for 0% -> 0%
where the time goes in v1:
time: 428 us; the launch traced here: 421 us
  waiting for transfers between devices  156 us (36%)
  matrix products  94.7 us (22%)
  local copies, waits for them, and re-layouts  54.2 us (13%)
  blocking collectives  51.8 us (12%)
  starting transfers between devices  22.8 us (5%)
  between operations  20.5 us (5%)
  other arithmetic  20.1 us (5%)
    all_gather x5, waiting for transfers between devices, by_axis(): array = jnp.sum(lax.all_gather(array, axis), axis=0)  143 us
    pmax x5, blocking collectives, one_axis_at_a_time(): array = lax.pmax(array, axis)  51.8 us
    dynamic_update_slice x2, local copies, waits for them, and re-layouts, tile_gradient(): lax.dynamic_update_slice(gradient, current + pieces[position], start_at)  27.9 us
    dot_general x6, matrix products, transform(): ic = jnp.einsum('byx,xk->byk', imag_part, cosine, precision=high)  12.9 us
    dot_general x6, matrix products, transform(): rc = jnp.einsum('byx,xk->byk', real_part, cosine, precision=high)  12.6 us
    dot_general x6, matrix products, transform(): jnp.einsum('ky,byx->bkx', sine_tab, mid_im, precision=high)  12.4 us
    dot_general x6, matrix products, transform(): isn = jnp.einsum('byx,xk->byk', imag_part, sine_tab, precision=high)  11.7 us
    dot_general x6, matrix products, transform(): rs = jnp.einsum('byx,xk->byk', real_part, sine_tab, precision=high)  11.7 us
  transfers between devices with their start and end apart: 13, of which 9 were waited for; matrix products, arithmetic and copies ran while one was open for 11% of the time, Pallas kernels for 0%

profile of v1, /device:TPU:8, one launch (start us, length us, event | category | flops | bytes accessed | tf_op | source)
XLA Modules:
  0.0 420.8 jit_solution(17112469551110878832)
XLA Ops:
  19.2 3.4 collective-permute-start.2
  22.6 4.6 %collective-permute-start.3 = (f32[2,2,320,32]{2,3,1,0:T(8,128)S(1)}, f32[2,2,320,32]{2,3,1,0:T(8,128)S(1)}, u32[]{:S(2)}, u32[]{:S(2)}) collective-permute-start(f32[2,2,320,32]{2,3,1,0:T(8,128)S(1)} %get-tuple-element.85), channel_id=1, source_target_pairs={{1,0},{2,1},{3,2},{4,3},{5,4},{6,5},{7,6},{8,7},{9,8},{10,9},{11,1... | collective-permute-start | bytes 491528 | tf_op jit(solution)/shard_map/ppermute | solution.py:30
  32.2 11.6 %while.5 = (s32[]{:T(128)}, f32[2,2,320,320]{2,3,1,0:T(8,128)S(1)}, s32[2,4]{1,0:T(2,128)S(1)}, f32[2,2,2,256,256]{3,4,0,2,1:T(8,128)}, s32[]{:T(128)}) while((s32[]{:T(128)}, f32[2,2,320,320]{2,3,1,0:T(8,128)S(1)}, s32[2,4]{1,0:T(2,128)S(1)}, f32[2,2,2,256,256]{3,4,0,2,1:T(8,128)}, s32[]{:T(128)}) %tuple.63), condition=%wide.while_cond.4, body=%wide.while_body.4.sunk | while | flops 2 | bytes 21496496 | solution.py:107
  43.8 3.4 fusion.112
  47.2 3.2 fusion.116
  80.5 2.3 convolution_add_fusion.3
  93.9 2.1 fusion.88
  105.4 2.2 add_bitcast_fusion
  116.8 2.3 fusion.82
  136.0 2.9 fusion.38
  140.0 69.2 %all-gather.11.cloned.1.call-done = f32[8,256,256]{2,1,0:T(8,128)} async-done(((f32[2,256,256]{2,1,0:T(8,128)}), f32[8,256,256]{2,1,0:T(8,128)}) %all-gather.11.cloned.1.call-update) | async-done | bytes 2097168 | tf_op jit(solution)/shard_map/all_gather | solution.py:39
  209.2 2.6 reduce_sum.65
  211.9 13.5 %all-gather.13.cloned.1.call-done = f32[4,256,256]{2,1,0:T(8,128)} async-done(((f32[2,256,256]{2,1,0:T(8,128)}), f32[4,256,256]{2,1,0:T(8,128)}) %all-gather.13.cloned.1.call-update) | async-done | bytes 1048592 | tf_op jit(solution)/shard_map/all_gather | solution.py:39
  225.4 2.2 reduce_sum.66
  227.7 27.8 %all-gather.15.cloned.1.call-done = f32[4,256,256]{2,1,0:T(8,128)} async-done(((f32[2,256,256]{2,1,0:T(8,128)}), f32[4,256,256]{2,1,0:T(8,128)}) %all-gather.15.cloned.1.call-update) | async-done | bytes 1048592 | tf_op jit(solution)/shard_map/all_gather | solution.py:39
  255.5 2.1 reduce_sum.67
  257.7 32.9 %all-gather.17.cloned.1.call-done = f32[8,256,256]{2,1,0:T(8,128)} async-done(((f32[2,256,256]{2,1,0:T(8,128)}), f32[8,256,256]{2,1,0:T(8,128)}) %all-gather.17.cloned.1.call-update) | async-done | bytes 2097168 | tf_op jit(solution)/shard_map/all_gather | solution.py:39
  290.6 2.6 reduce_sum.68
  300.4 14.1 %dynamic_update_slice.6 = f32[2,2,320,320]{2,3,1,0:T(8,128)S(1)} dynamic-update-slice(f32[2,2,320,320]{2,3,1,0:T(8,128)S(1)} %broadcast_in_dim.2, f32[2,2,256,256]{2,3,1,0:T(8,128)} %fusion.25, s32[]{:T(128)} %constant.162.clone.1, s32[]{:T(128)} %constant.162.clone.1, s32[]{:T(128)S(6)} %select_n.155, s32[]{:T(128)S(6)} %select_n.156) | dynamic-update-slice | bytes 2097156 | tf_op jit(solution)/shard_map/dynamic_update_slice | solution.py:136
  314.6 2.4 fusion.27
  317.0 13.8 %dynamic_update_slice.7 = f32[2,2,320,320]{2,3,1,0:T(8,128)S(1)} dynamic-update-slice(f32[2,2,320,320]{2,3,1,0:T(8,128)S(1)} %dynamic_update_slice.6, f32[2,2,256,256]{2,3,1,0:T(8,128)} %fusion.27, s32[]{:T(128)} %constant.162.clone.1, s32[]{:T(128)} %constant.162.clone.1, s32[]{:T(128)S(6)} %select_n.157, s32[]{:T(128)S(6)} %select_n.158) | dynamic-update-slice | bytes 2097156 | tf_op jit(solution)/shard_map/dynamic_update_slice | solution.py:136
  330.8 5.0 %collective-permute-start.4 = (f32[2,2,32,320]{3,2,1,0:T(8,128)S(1)}, f32[2,2,32,320]{3,2,1,0:T(8,128)S(1)}, u32[]{:S(2)}, u32[]{:S(2)}) collective-permute-start(f32[2,2,32,320]{3,2,1,0:T(8,128)S(1)} %get-tuple-element.87), channel_id=1, source_target_pairs={{1,0},{2,1},{3,2},{4,3},{5,4},{6,5},{7,6},{8,7},{9,8},{10,9},{11,1... | collective-permute-start | bytes 491528 | tf_op jit(solution)/shard_map/ppermute | solution.py:17
  337.9 2.4 collective-permute-done.4
  340.3 6.3 %collective-permute-done.5 = f32[2,2,32,320]{3,2,1,0:T(8,128)S(1)} collective-permute-done((f32[2,2,32,320]{3,2,1,0:T(8,128)S(1)}, f32[2,2,32,320]{3,2,1,0:T(8,128)S(1)}, u32[]{:S(2)}, u32[]{:S(2)}) %collective-permute-start.5) | collective-permute-done | bytes 163872 | tf_op jit(solution)/shard_map/ppermute | solution.py:17
  348.5 3.3 collective-permute-start.7
  351.9 2.4 scatter-add.16
  354.3 2.3 scatter-add.19
  357.4 26.3 %pmax.35 = f32[]{:T(128)} all-reduce(f32[]{:T(128)} %fusion.29), channel_id=1, replica_groups=mesh['row_0'=4,'row_1'=2,'col_0'=2,'col_1'=4,'col_2'=4] {'row_0'}, use_global_device_ids=true, to_apply=%region_1.2 | all-reduce | flops 1 | bytes 8 | tf_op jit(solution)/shard_map/pmax | solution.py:45
  383.7 3.1 pmax.36
  386.8 5.5 %pmax.37 = f32[]{:T(128)} all-reduce(f32[]{:T(128)} %pmax.36), channel_id=1, replica_groups=mesh['row_0'=4,'row_1'=2,'col_0'=2,'col_1'=4,'col_2'=4] {'col_0'}, use_global_device_ids=true, to_apply=%region_3.4 | all-reduce | flops 1 | bytes 8 | tf_op jit(solution)/shard_map/pmax | solution.py:45
  392.3 8.5 %pmax.38 = f32[]{:T(128)} all-reduce(f32[]{:T(128)} %pmax.37), channel_id=1, replica_groups=mesh['row_0'=4,'row_1'=2,'col_0'=2,'col_1'=4,'col_2'=4] {'col_1'}, use_global_device_ids=true, to_apply=%region_4.5 | all-reduce | flops 1 | bytes 8 | tf_op jit(solution)/shard_map/pmax | solution.py:45
  400.8 8.3 %pmax.39 = f32[]{:T(128)} all-reduce(f32[]{:T(128)} %pmax.38), channel_id=1, replica_groups=mesh['row_0'=4,'row_1'=2,'col_0'=2,'col_1'=4,'col_2'=4] {'col_2'}, use_global_device_ids=true, to_apply=%region_5.6 | all-reduce | flops 1 | bytes 8 | tf_op jit(solution)/shard_map/pmax | solution.py:45
  (142 shorter events, 116.7 us)
Async XLA Ops:
  7.2 6.2 %copy-start.11 = (f32[2,256,256]{2,1,0:T(8,128)S(1)}, f32[2,256,256]{2,1,0:T(8,128)}, u32[]{:S(2)}) copy-start(f32[2,256,256]{2,1,0:T(8,128)} %param.13) | copy-start | bytes 1572868
  7.2 202.0 %all-gather.11.cloned.1.call-start = ((), (), s32[]{:S(2)}) async-start(), calls=%async_computation | async-start | bytes 2621440 | tf_op jit(solution)/shard_map/all_gather | solution.py:39
  8.8 21.5 %copy-start.2 = (f32[2,2,256,256]{2,3,1,0:T(8,128)}, f32[2,2,256,256]{2,3,1,0:T(8,128)S(1)}, u32[]{:S(2)}) copy-start(f32[2,2,256,256]{2,3,1,0:T(8,128)S(1)} %copy.124) | copy-start | bytes 3145732
  10.1 8.1 %copy-start.14 = (s32[1,1,2,2]{3,2,1,0:T(2,128)S(1)}, s32[1,1,2,2]{3,2,1,0:T(2,128)}, u32[]{:S(2)}) copy-start(s32[1,1,2,2]{3,2,1,0:T(2,128)} %param.14) | copy-start | bytes 52
  10.1 8.1 %collective-permute-start = (f32[2,2,32,256]{2,3,1,0:T(8,128)}, f32[2,2,32,256]{2,3,1,0:T(8,128)S(1)}, u32[]{:S(2)}, u32[]{:S(2)}) collective-permute-start(f32[2,2,32,256]{2,3,1,0:T(8,128)} %get-tuple-element.96), channel_id=1, source_target_pairs={{0,32},{32,64},{64,96},{96,128},{128,160},{160,192},{192,224},{1,3... | collective-permute-start | bytes 393224 | tf_op jit(solution)/shard_map/ppermute | solution.py:28
  12.0 7.0 %collective-permute-start.1 = (f32[2,2,32,256]{2,3,1,0:T(8,128)}, f32[2,2,32,256]{2,3,1,0:T(8,128)S(1)}, u32[]{:S(2)}, u32[]{:S(2)}) collective-permute-start(f32[2,2,32,256]{2,3,1,0:T(8,128)} %get-tuple-element.97), channel_id=1, source_target_pairs={{32,0},{64,32},{96,64},{128,96},{160,128},{192,160},{224,192},{33,... | collective-permute-start | bytes 393224 | tf_op jit(solution)/shard_map/ppermute | solution.py:30
  18.2 10.7 %copy-start.9 = (f32[2,2,32,256]{2,3,1,0:T(8,128)}, f32[2,2,32,256]{2,3,1,0:T(8,128)S(1)}, u32[]{:S(2)}) copy-start(f32[2,2,32,256]{2,3,1,0:T(8,128)S(1)} %collective-permute-done) | copy-start | bytes 393220
  19.0 9.9 %copy-start.10 = (f32[2,2,32,256]{2,3,1,0:T(8,128)}, f32[2,2,32,256]{2,3,1,0:T(8,128)S(1)}, u32[]{:S(2)}) copy-start(f32[2,2,32,256]{2,3,1,0:T(8,128)S(1)} %collective-permute-done.1) | copy-start | bytes 393220
  19.2 9.7 %collective-permute-start.2 = (f32[2,2,320,32]{2,3,1,0:T(8,128)S(1)}, f32[2,2,320,32]{2,3,1,0:T(8,128)S(1)}, u32[]{:S(2)}, u32[]{:S(2)}) collective-permute-start(f32[2,2,320,32]{2,3,1,0:T(8,128)S(1)} %get-tuple-element.84), channel_id=1, source_target_pairs={{0,1},{1,2},{2,3},{3,4},{4,5},{5,6},{6,7},{7,8},{8,9},{9,10},{10,1... | collective-permute-start | bytes 491528 | tf_op jit(solution)/shard_map/ppermute | solution.py:28
  22.6 7.7 %collective-permute-start.3 = (f32[2,2,320,32]{2,3,1,0:T(8,128)S(1)}, f32[2,2,320,32]{2,3,1,0:T(8,128)S(1)}, u32[]{:S(2)}, u32[]{:S(2)}) collective-permute-start(f32[2,2,320,32]{2,3,1,0:T(8,128)S(1)} %get-tuple-element.85), channel_id=1, source_target_pairs={{1,0},{2,1},{3,2},{4,3},{5,4},{6,5},{7,6},{8,7},{9,8},{10,9},{11,1... | collective-permute-start | bytes 491528 | tf_op jit(solution)/shard_map/ppermute | solution.py:30
  32.2 1.3 copy-start
  35.8 1.9 copy-start.1
  37.8 1.3 copy-start
  41.4 1.9 copy-start.1
  43.8 6.6 %copy-start.6 = (f32[256,256]{0,1:T(8,128)S(1)}, f32[256,256]{0,1:T(8,128)}, u32[]{:S(2)}) copy-start(f32[256,256]{0,1:T(8,128)} %copy.64) | copy-start | bytes 786436
  43.8 6.6 %copy-start.7 = (f32[256,256]{0,1:T(8,128)S(1)}, f32[256,256]{0,1:T(8,128)}, u32[]{:S(2)}) copy-start(f32[256,256]{0,1:T(8,128)} %copy.71) | copy-start | bytes 786436
  43.8 6.6 %copy-start.8 = (f32[2,2,2,256,256]{3,4,0,2,1:T(8,128)S(1)}, f32[2,2,2,256,256]{3,4,0,2,1:T(8,128)}, u32[]{:S(2)}) copy-start(f32[2,2,2,256,256]{3,4,0,2,1:T(8,128)} %get-tuple-element.57) | copy-start | bytes 6291460
  86.4 5.5 %copy-start.4 = (f32[1,1,2,256,256]{3,4,2,1,0:T(8,128)S(1)}, f32[1,1,2,256,256]{3,4,2,1,0:T(8,128)}, u32[]{:S(2)}) copy-start(f32[1,1,2,256,256]{3,4,2,1,0:T(8,128)} %copy.98) | copy-start | bytes 1572868
  140.0 85.4 %all-gather.13.cloned.1.call-start = ((), (), s32[]{:S(2)}) async-start(), calls=%async_computation.1 | async-start | bytes 1572864 | tf_op jit(solution)/shard_map/all_gather | solution.py:39
  211.8 43.7 %all-gather.15.cloned.1.call-start = ((), (), s32[]{:S(2)}) async-start(), calls=%async_computation.2 | async-start | bytes 1572864 | tf_op jit(solution)/shard_map/all_gather | solution.py:39
  227.6 63.0 %all-gather.17.cloned.1.call-start = ((), (), s32[]{:S(2)}) async-start(), calls=%async_computation.3 | async-start | bytes 2621440 | tf_op jit(solution)/shard_map/all_gather | solution.py:39
  257.6 41.2 %copy-start.13 = (f32[2,1,256,256]{2,3,0,1:T(8,128)S(1)}, f32[2,1,256,256]{2,3,0,1:T(8,128)}, u32[]{:S(2)}) copy-start(f32[2,1,256,256]{2,3,0,1:T(8,128)} %get-tuple-element.93) | copy-start | bytes 1572868
  257.7 153.7 %all-gather.19.cloned.1.call-start = ((), (), s32[]{:S(2)}) async-start(), calls=%async_computation.4 | async-start | bytes 2621440 | tf_op jit(solution)/shard_map/all_gather | solution.py:39
  299.0 1.3 copy-start.5
  330.8 9.4 %collective-permute-start.4 = (f32[2,2,32,320]{3,2,1,0:T(8,128)S(1)}, f32[2,2,32,320]{3,2,1,0:T(8,128)S(1)}, u32[]{:S(2)}, u32[]{:S(2)}) collective-permute-start(f32[2,2,32,320]{3,2,1,0:T(8,128)S(1)} %get-tuple-element.87), channel_id=1, source_target_pairs={{1,0},{2,1},{3,2},{4,3},{5,4},{6,5},{7,6},{8,7},{9,8},{10,9},{11,1... | collective-permute-start | bytes 491528 | tf_op jit(solution)/shard_map/ppermute | solution.py:17
  335.9 10.7 %collective-permute-start.5 = (f32[2,2,32,320]{3,2,1,0:T(8,128)S(1)}, f32[2,2,32,320]{3,2,1,0:T(8,128)S(1)}, u32[]{:S(2)}, u32[]{:S(2)}) collective-permute-start(f32[2,2,32,320]{3,2,1,0:T(8,128)S(1)} %get-tuple-element.86), channel_id=1, source_target_pairs={{0,1},{1,2},{2,3},{3,4},{4,5},{5,6},{6,7},{7,8},{8,9},{9,10},{10,1... | collective-permute-start | bytes 491528 | tf_op jit(solution)/shard_map/ppermute | solution.py:17
  346.9 4.9 %collective-permute-start.6 = (f32[2,2,32,256]{2,3,1,0:T(8,128)S(1)}, f32[2,2,32,256]{2,3,1,0:T(8,128)S(1)}, u32[]{:S(2)}, u32[]{:S(2)}) collective-permute-start(f32[2,2,32,256]{2,3,1,0:T(8,128)S(1)} %get-tuple-element.89), channel_id=1, source_target_pairs={{32,0},{64,32},{96,64},{128,96},{160,128},{192,160},{224,192},{33,... | collective-permute-start | bytes 393224 | tf_op jit(solution)/shard_map/ppermute | solution.py:17
  348.5 5.8 %collective-permute-start.7 = (f32[2,2,32,256]{2,3,1,0:T(8,128)S(1)}, f32[2,2,32,256]{2,3,1,0:T(8,128)S(1)}, u32[]{:S(2)}, u32[]{:S(2)}) collective-permute-start(f32[2,2,32,256]{2,3,1,0:T(8,128)S(1)} %get-tuple-element.88), channel_id=1, source_target_pairs={{0,32},{32,64},{64,96},{96,128},{128,160},{160,192},{192,224},{1,3... | collective-permute-start | bytes 393224 | tf_op jit(solution)/shard_map/ppermute | solution.py:17
  354.3 55.6 %copy-start.3 = (f32[2,2,256,256]{2,3,1,0:T(8,128)S(1)}, f32[2,2,256,256]{2,3,1,0:T(8,128)}, u32[]{:S(2)}) copy-start(f32[2,2,256,256]{2,3,1,0:T(8,128)} %copy-done.2) | copy-start | bytes 3145732
  410.0 3.1 copy-start.12
Sparse Core Ops, SparseCore 0:
  140.1 69.0 all-gather.10
  211.9 13.4 all-gather.12
  227.7 27.7 all-gather.14
  257.8 32.7 all-gather.16
  293.3 34.2 all-gather.18
